TPU v7x, 512 devices: a whole 4x8x8 slice. The times are simulated.
512 devices in a mesh: row: 32 (over x, y), col: 16 (over z, core).
Axes of the slice: x: 4, y: 8, z: 8, core: 2. Of those that a mesh axis runs over, the one named last changes fastest.
Arguments:
- window: float32 [32, 2048, 16, 256], P('row', None, 'col'), may hold values from -7 to 8, as said below
Outputs:
- factored: float32 [32, 2048, 16, 256], P('row', None, 'col')
Inputs may be any that keep to these rules, and one draw needn't show every extreme that they name: `window`: entries above the diagonal are never read. The leading 2 * 128 by 256 block (lower triangle mirrored) is positive definite, with smallest eigenvalue 1 or more.
All inputs are finite; a program needn't handle non-finite values.
Results may differ from a plain program's by a relative error of at most 0.00028.
Values sent between devices are 32-bit elements; how exact they have to be, the bound alone decides.
A program may use at most 64 MiB of HBM per device.

v0:
```python
import jax
import jax.numpy as jnp
from jax import lax
from jax.sharding import PartitionSpec as P

NB = 128


def unmix_cols(gathered, col_count):
    height = gathered.shape[0]
    width = gathered.shape[1]
    return (
        gathered.reshape(height, col_count, width // col_count)
        .transpose(0, 2, 1)
        .reshape(height, width)
    )


def solve_rows(factor, rows_in):
    return jax.scipy.linalg.solve_triangular(factor, rows_in.T, lower=True).T


def body(window):
    blocks = window[0, :, 0, :]
    local_rows = blocks.shape[0]
    local_cols = blocks.shape[1]
    row_count = lax.axis_size("row")
    col_count = lax.axis_size("col")
    row_index = lax.axis_index("row")
    col_index = lax.axis_index("col")
    tile_height = NB // row_count
    tile_width = NB // col_count
    head_rows = local_cols * col_count // row_count
    groups = row_count // col_count
    for panel_step in range(2):
        first_col = panel_step * tile_width
        after_col = first_col + tile_width
        first_row = panel_step * tile_height
        tile_piece = blocks[first_row : first_row + tile_height, first_col:after_col]
        tile_wide = lax.all_gather(tile_piece, "col", axis=1, tiled=True)
        tile_full = lax.all_gather(tile_wide, "row", axis=0, tiled=True)
        tile_full = tile_full.reshape(row_count, tile_height, NB).transpose(1, 0, 2).reshape(NB, NB)
        diag_tile = unmix_cols(tile_full, col_count)
        symmetric = jnp.tril(diag_tile) + jnp.tril(diag_tile, -1).T
        factor = jnp.tril(jnp.linalg.cholesky(symmetric))
        panel_mine = blocks[:, first_col:after_col]
        gathered = lax.all_gather(panel_mine, "col", axis=1, tiled=True)
        solved = solve_rows(factor, unmix_cols(gathered, col_count))
        diag_rows = lax.dynamic_index_in_dim(
            factor.reshape(tile_height, row_count, NB), row_index, 1, False
        )
        panel_rows = jnp.concatenate(
            [jnp.zeros((first_row, NB), jnp.float32), diag_rows, solved[first_row + tile_height :]],
            0,
        )
        own_cols = lax.dynamic_index_in_dim(
            panel_rows.reshape(local_rows, tile_width, col_count), col_index, 2, False
        )
        sending = panel_rows[:head_rows]
        all_rows = lax.all_gather(sending, "row", axis=0, tiled=True)
        picked = lax.dynamic_index_in_dim(
            all_rows.reshape(groups, col_count, head_rows, NB), col_index, 1, False
        )
        col_rows = picked.transpose(1, 0, 2).reshape(local_cols, NB)
        update = jnp.dot(panel_rows, col_rows[after_col:].T, precision=lax.Precision.HIGHEST)
        trailing = blocks[:, after_col:] - update
        blocks = jnp.concatenate([blocks[:, :first_col], own_cols, trailing], 1)
    global_rows = jnp.arange(local_rows)[:, None] * row_count + row_index
    global_cols = jnp.arange(local_cols)[None, :] * col_count + col_index
    lower_mask = global_rows >= global_cols
    result = jnp.where(lower_mask, blocks, 0.0)
    return result[None, :, None, :]


def solution(mesh):
    in_specs = (P("row", None, "col", None),)
    out_specs = P("row", None, "col", None)
    return jax.shard_map(body, mesh=mesh, in_specs=in_specs, out_specs=out_specs, check_vma=False)
```

profile of v0, /device:TPU:14, one launch (start us, length us, event | category | flops | bytes accessed | tf_op | source)
XLA Modules:
  0.0 380.1 jit_solution(15478815313496594066)
XLA Ops:
  6.5 4.6 %copy.51 = f32[1,2048,1,256]{1,3,2,0:T(8,128)S(1)} copy(f32[1,2048,1,256]{3,2,1,0:T(1,128)} %param.4) | data formatting | bytes 4194304 | tf_op args[0]
  11.1 0.6 slice.65
  11.9 23.2 %all-gather = f32[16,8,4]{1,2,0:T(4,128)S(1)} all-gather(f32[1,8,4]{1,2,0:T(4,128)S(1)} %bitcast.136), channel_id=1, replica_groups=mesh['row'=32,'col'=16] {'col'}, dimensions={0}, use_global_device_ids=true | all-gather | bytes 2176 | tf_op jit(solution)/shard_map/all_gather | solution.py:40
  35.2 48.2 %all-gather.1 = f32[32,4,128]{2,1,0:T(4,128)S(1)} all-gather(f32[1,4,128]{2,1,0:T(4,128)S(1)} %bitcast.137), channel_id=1, replica_groups=mesh['row'=32,'col'=16] {'row'}, dimensions={0}, use_global_device_ids=true | all-gather | bytes 67584 | tf_op jit(solution)/shard_map/all_gather | solution.py:41
  83.4 0.2 copy.54
  83.6 0.2 reshape_reshape.6
  84.1 11.7 %cholesky.44 = f32[128,128]{1,0:T(8,128)S(1)} custom-call(f32[128,128]{1,0:T(8,128)S(1)} %fusion.8), custom_call_target="Cholesky" | custom-call | tf_op jit(solution)/shard_map/jit(cholesky)/cholesky | solution.py:45
  96.0 0.7 compare_reduce_fusion.1
  96.7 0.6 select_bitcast_fusion.1
  97.7 9.8 %custom-call.6 = f32[1,128,128]{1,2,0:T(8,128)S(1)} custom-call(f32[1,128,128]{2,1,0:T(8,128)S(1)} %copy.63), custom_call_target="InvertDiagBlocksLowerTriangular" | custom-call | tf_op jit(solution)/shard_map/jit(_solve_triangular)/triangular_solve | solution.py:20
  107.5 1.8 copy.64
  109.4 1.1 convolution_bitcast_fusion.1
  110.4 0.3 slice.66
  110.7 0.7 pad_maximum_fusion
  111.5 76.0 %all-gather.11.cloned.1.call-done = f32[4096,128]{0,1:T(8,128)} async-done(((f32[128,128]{0,1:T(8,128)}), f32[4096,128]{0,1:T(8,128)}) %all-gather.11.cloned.1.call-update) | async-done | bytes 2097168 | tf_op jit(solution)/shard_map/all_gather | solution.py:60
  187.6 2.0 copy.88
  189.5 0.1 constant_dynamic-slice_fusion.2
  189.7 0.1 copy.67
  189.8 1.9 convolution_subtract_fusion
  191.7 1.3 copy-done
  193.0 0.6 slice.70
  193.7 0.2 all-gather.15.cloned.1.call-start
  193.9 0.1 copy.75
  194.0 0.8 slice_bitcast_fusion
  194.9 18.1 %all-gather.2 = f32[16,8,4]{1,2,0:T(4,128)S(1)} all-gather(f32[1,8,4]{1,2,0:T(4,128)S(1)} %bitcast.138), channel_id=1, replica_groups=mesh['row'=32,'col'=16] {'col'}, dimensions={0}, use_global_device_ids=true | all-gather | bytes 2176 | tf_op jit(solution)/shard_map/all_gather | solution.py:40
  213.1 46.1 %all-gather.3 = f32[32,4,128]{2,1,0:T(4,128)S(1)} all-gather(f32[1,4,128]{2,1,0:T(4,128)S(1)} %bitcast.139), channel_id=1, replica_groups=mesh['row'=32,'col'=16] {'row'}, dimensions={0}, use_global_device_ids=true | all-gather | bytes 67584 | tf_op jit(solution)/shard_map/all_gather | solution.py:41
  259.2 0.2 copy.70
  259.4 0.2 reshape_reshape.7
  259.9 11.7 %cholesky.55 = f32[128,128]{1,0:T(8,128)S(1)} custom-call(f32[128,128]{1,0:T(8,128)S(1)} %fusion.6), custom_call_target="Cholesky" | custom-call | tf_op jit(solution)/shard_map/jit(cholesky)/cholesky | solution.py:45
  271.6 0.6 compare_reduce_fusion
  272.3 0.6 select_bitcast_fusion
  272.8 9.8 %custom-call.7 = f32[1,128,128]{1,2,0:T(8,128)S(1)} custom-call(f32[1,128,128]{2,1,0:T(8,128)S(1)} %get-tuple-element.6), custom_call_target="InvertDiagBlocksLowerTriangular" | custom-call | tf_op jit(solution)/shard_map/jit(_solve_triangular)/triangular_solve | solution.py:20
  282.8 1.8 copy.77
  284.7 1.1 convolution_bitcast_fusion
  285.7 0.3 slice.71
  286.1 1.0 concatenate.45
  287.0 0.7 slice.73
  287.9 0.2 fusion.4
  288.2 0.1 copy.78
  288.3 0.6 copy.79
  288.9 0.7 concatenate.43
  289.7 75.8 %all-gather.15.cloned.1.call-done = f32[4096,128]{0,1:T(8,128)} async-done(((f32[128,128]{0,1:T(8,128)}), f32[4096,128]{0,1:T(8,128)}) %all-gather.15.cloned.1.call-update) | async-done | bytes 2097168 | tf_op jit(solution)/shard_map/all_gather | solution.py:60
  365.5 2.1 copy.89
  367.6 0.1 constant_dynamic-slice_fusion
  367.8 0.1 copy.81
  368.0 1.8 fusion
  369.8 0.2 maximum_select_fusion
  370.0 3.6 copy.82
  (53 shorter events, 2.1 us)
Async XLA Ops:
  6.5 101.0 %all-gather.9.cloned.1.call-start = ((), (), s32[]{:S(2)}) async-start(), calls=%async_computation | async-start | bytes 1114112 | tf_op jit(solution)/shard_map/all_gather | solution.py:47
  11.8 175.8 %all-gather.11.cloned.1.call-start = ((), (), s32[]{:S(2)}) async-start(), calls=%async_computation.1 | async-start | bytes 2162688 | tf_op jit(solution)/shard_map/all_gather | solution.py:60
  111.5 171.3 %all-gather.13.cloned.1.call-start = ((), (), s32[]{:S(2)}) async-start(), calls=%async_computation.2 | async-start | bytes 1114112 | tf_op jit(solution)/shard_map/all_gather | solution.py:47
  191.7 1.3 copy-start
  193.7 171.9 %all-gather.15.cloned.1.call-start = ((), (), s32[]{:S(2)}) async-start(), calls=%async_computation.3 | async-start | bytes 2162688 | tf_op jit(solution)/shard_map/all_gather | solution.py:60
  287.0 2.6 copy-start.2
  365.5 2.4 copy-start.1
  365.5 2.5 copy-start.3
Sparse Core Ops, SparseCore 0:
  11.9 46.4 all-gather.8
  111.6 75.8 all-gather.10
  193.8 41.1 all-gather.12
  287.9 77.6 all-gather.14
where the time goes:
time: 380 us
  waiting for transfers between devices  152 us (40%)
  blocking collectives  136 us (36%)
  other arithmetic  47.1 us (12%)
  local copies, waits for them, and re-layouts  25.8 us (7%)
  between operations  13.6 us (4%)
  matrix products  5.78 us (2%)
    all_gather x2, waiting for transfers between devices, body(): all_rows = lax.all_gather(sending, 'row', axis=0, tiled=True)  152 us
    all_gather x2, blocking collectives, body(): tile_full = lax.all_gather(tile_wide, 'row', axis=0, tiled=True)  94.3 us
    all_gather x2, blocking collectives, body(): tile_wide = lax.all_gather(tile_piece, 'col', axis=1, tiled=True)  41.3 us
    another operation x6, other arithmetic, body(): factor = jnp.tril(jnp.linalg.cholesky(symmetric))  24.9 us
    another operation x4, other arithmetic, solve_rows(): return jax.scipy.linalg.solve_triangular(factor, rows_in.T, lower=True).T  20.8 us
    unnamed x18, local copies, waits for them, and re-layouts  11.1 us
  transfers between devices with their start and end apart: 4, of which 2 were waited for; matrix products, arithmetic and copies ran while one was open for 13% of the time, Pallas kernels for 0%

commit v1 on v0

--- a/solution.py
+++ b/solution.py
@@ -4,6 +4,36 @@
 from jax.sharding import PartitionSpec as P
 
 NB = 128
+
+
+def measure_tasks(vals, lane_axis):
+    spare = lax.psum(1, axis_name=lane_axis)
+    raw_out = lax.axis_index(lane_axis)
+    x_new, reached, formed = (spare, raw_out, vals.shape[1])
+    windows = tuple((at * x_new if src_i == 1 else at for src_i, at in enumerate(vals.shape)))
+    parts_out = lax.dynamic_update_slice_in_dim(
+        jnp.zeros(windows, vals.dtype), vals, reached * formed, axis=1
+    )
+    item_now = r2 = vals
+    for it in range(1, x_new // 2 + 1):
+        item_now = lax.ppermute(
+            item_now,
+            axis_name=lane_axis,
+            perm=tuple(((src_i, (src_i + 1) % x_new) for src_i in range(x_new))),
+        )
+        parts_out = lax.dynamic_update_slice_in_dim(
+            parts_out, item_now, (reached - it) % x_new * formed, axis=1
+        )
+        if 2 * it < x_new:
+            r2 = lax.ppermute(
+                r2,
+                axis_name=lane_axis,
+                perm=tuple(((src_i, (src_i - 1) % x_new) for src_i in range(x_new))),
+            )
+            parts_out = lax.dynamic_update_slice_in_dim(
+                parts_out, r2, (reached + it) % x_new * formed, axis=1
+            )
+    return parts_out
 
 
 def unmix_cols(gathered, col_count):
@@ -37,7 +67,7 @@
         after_col = first_col + tile_width
         first_row = panel_step * tile_height
         tile_piece = blocks[first_row : first_row + tile_height, first_col:after_col]
-        tile_wide = lax.all_gather(tile_piece, "col", axis=1, tiled=True)
+        tile_wide = measure_tasks(tile_piece, "col")
         tile_full = lax.all_gather(tile_wide, "row", axis=0, tiled=True)
         tile_full = tile_full.reshape(row_count, tile_height, NB).transpose(1, 0, 2).reshape(NB, NB)
         diag_tile = unmix_cols(tile_full, col_count)

time: 380 us -> 422 us (1.11)
  starting transfers between devices: 0.31 us -> 47.3 us
  blocking collectives: 136 us -> 94.4 us
  waiting for transfers between devices: 152 us -> 179 us
  local copies, waits for them, and re-layouts: 25.8 us -> 34 us
    ppermute x0 -> x30, starting transfers between devices: none -> 47 us  [the longest x14 46.9 us: measure_tasks(): lax.ppermute(r2, axis_name=lane_axis, perm=tuple(((src_i, (src_i - 1) % x...]
    all_gather x2 -> x0, blocking collectives: 41.3 us -> none  [body(): tile_wide = lax.all_gather(tile_piece, 'col', axis=1, tiled=True)]
    ppermute x0 -> x30, waiting for transfers between devices: none -> 22.3 us  [the longest x16 21.3 us: measure_tasks(): lax.ppermute(item_now, axis_name=lane_axis, perm=tuple(((src_i, (src_i +...]
    dynamic_update_slice x0 -> x32, local copies, waits for them, and re-layouts: none -> 5.86 us  [the longest x16 3.03 us: measure_tasks(): lax.dynamic_update_slice_in_dim(parts_out, item_now, (reached - it) % x_n...]
    all_gather x2, waiting for transfers between devices: 152 us -> 157 us  [body(): all_rows = lax.all_gather(sending, 'row', axis=0, tiled=True)]
    unnamed x18 -> x14, local copies, waits for them, and re-layouts: 11.1 us -> 10 us
  transfers between devices with their start and end apart: 4 -> 34, of which waited for: 2 -> 22; matrix products, arithmetic and copies ran while one was open for 13% -> 14% of each run, Pallas kernels for 0% -> 0%
where the time goes in v1:
time: 422 us
  waiting for transfers between devices  179 us (42%)
  blocking collectives  94.4 us (22%)
  starting transfers between devices  47.3 us (11%)
  other arithmetic  47.2 us (11%)
  local copies, waits for them, and re-layouts  34 us (8%)
  between operations  13.7 us (3%)
  matrix products  5.78 us (1%)
    all_gather x2, waiting for transfers between devices, body(): all_rows = lax.all_gather(sending, 'row', axis=0, tiled=True)  157 us
    all_gather x2, blocking collectives, body(): tile_full = lax.all_gather(tile_wide, 'row', axis=0, tiled=True)  94.4 us
    ppermute x14, starting transfers between devices, measure_tasks(): lax.ppermute(r2, axis_name=lane_axis, perm=tuple(((src_i, (src_i - 1) % x...  46.9 us
    another operation x6, other arithmetic, body(): factor = jnp.tril(jnp.linalg.cholesky(symmetric))  24.9 us
    ppermute x16, waiting for transfers between devices, measure_tasks(): lax.ppermute(item_now, axis_name=lane_axis, perm=tuple(((src_i, (src_i +...  21.3 us
    another operation x4, other arithmetic, solve_rows(): return jax.scipy.linalg.solve_triangular(factor, rows_in.T, lower=True).T  20.9 us
    unnamed x14, local copies, waits for them, and re-layouts  10 us
  transfers between devices with their start and end apart: 34, of which 22 were waited for; matrix products, arithmetic and copies ran while one was open for 14% of the time, Pallas kernels for 0%

profile of v1, /device:TPU:14, one launch (start us, length us, event | category | flops | bytes accessed | tf_op | source)
XLA Modules:
  0.0 421.8 jit_solution(9144641120843667106)
XLA Ops:
  6.5 4.6 %copy.139 = f32[1,2048,1,256]{1,3,2,0:T(8,128)S(1)} copy(f32[1,2048,1,256]{3,2,1,0:T(1,128)} %param.4) | data formatting | bytes 4194304 | tf_op args[0]
  11.9 8.5 %collective-permute-start.1 = (f32[4,8]{0,1:T(8,128)S(1)}, f32[4,8]{0,1:T(8,128)S(1)}, u32[]{:S(2)}, u32[]{:S(2)}) collective-permute-start(f32[4,8]{0,1:T(8,128)S(1)} %slice.64), channel_id=1, source_target_pairs={{0,15},{1,0},{2,1},{3,2},{4,3},{5,4},{6,5},{7,6},{8,7},{9,8},{10,9... | collective-permute-start | bytes 392 | tf_op jit(solution)/shard_map/ppermute | solution.py:28
  20.5 1.1 collective-permute-done
  22.2 2.9 collective-permute-start.3
  25.0 1.1 collective-permute-done.2
  26.7 3.0 collective-permute-start.5
  29.6 1.0 collective-permute-done.4
  31.2 2.9 collective-permute-start.7
  34.2 1.0 collective-permute-done.6
  35.8 2.9 collective-permute-start.9
  38.7 1.0 collective-permute-done.8
  40.3 2.9 collective-permute-start.11
  43.2 1.0 collective-permute-done.10
  44.8 3.3 collective-permute-start.13
  49.7 3.5 collective-permute-done.14
  53.6 48.3 %all-gather = f32[32,4,128]{2,1,0:T(4,128)S(1)} all-gather(f32[1,4,128]{2,1,0:T(4,128)S(1)} %dynamic_update_slice.128), channel_id=1, replica_groups=mesh['row'=32,'col'=16] {'row'}, dimensions={0}, use_global_device_ids=true | all-gather | bytes 67584 | tf_op jit(solution)/shard_map/all_gather | solution.py:71
  102.5 11.7 %cholesky.44 = f32[128,128]{1,0:T(8,128)S(1)} custom-call(f32[128,128]{1,0:T(8,128)S(1)} %fusion.8), custom_call_target="Cholesky" | custom-call | tf_op jit(solution)/shard_map/jit(cholesky)/cholesky | solution.py:75
  115.8 9.8 %custom-call.6 = f32[1,128,128]{1,2,0:T(8,128)S(1)} custom-call(f32[1,128,128]{2,1,0:T(8,128)S(1)} %copy.165), custom_call_target="InvertDiagBlocksLowerTriangular" | custom-call | tf_op jit(solution)/shard_map/jit(_solve_triangular)/triangular_solve | solution.py:50
  125.9 1.8 copy.166
  127.8 1.1 convolution_bitcast_fusion.1
  129.9 78.0 %all-gather.9.cloned.1.call-done = f32[4096,128]{0,1:T(8,128)} async-done(((f32[128,128]{0,1:T(8,128)}), f32[4096,128]{0,1:T(8,128)}) %all-gather.9.cloned.1.call-update) | async-done | bytes 2097168 | tf_op jit(solution)/shard_map/all_gather | solution.py:90
  208.0 2.0 copy.204
  210.2 1.9 convolution_subtract_fusion
  212.1 1.3 copy-done
  215.3 3.0 collective-permute-start.16
  218.4 1.1 collective-permute-done.15
  220.0 2.9 collective-permute-start.18
  222.9 1.1 collective-permute-done.17
  224.6 3.0 collective-permute-start.20
  227.5 1.0 collective-permute-done.19
  229.1 2.9 collective-permute-start.22
  232.0 1.0 collective-permute-done.21
  233.6 2.9 collective-permute-start.24
  236.6 1.0 collective-permute-done.23
  238.2 3.0 collective-permute-start.26
  241.1 0.9 collective-permute-done.25
  242.7 2.9 collective-permute-start.28
  247.3 3.8 collective-permute-done.29
  251.4 46.1 %all-gather.1 = f32[32,4,128]{2,1,0:T(4,128)S(1)} all-gather(f32[1,4,128]{2,1,0:T(4,128)S(1)} %dynamic_update_slice.129), channel_id=1, replica_groups=mesh['row'=32,'col'=16] {'row'}, dimensions={0}, use_global_device_ids=true | all-gather | bytes 67584 | tf_op jit(solution)/shard_map/all_gather | solution.py:71
  298.2 11.7 %cholesky.55 = f32[128,128]{1,0:T(8,128)S(1)} custom-call(f32[128,128]{1,0:T(8,128)S(1)} %fusion.6), custom_call_target="Cholesky" | custom-call | tf_op jit(solution)/shard_map/jit(cholesky)/cholesky | solution.py:75
  311.3 9.8 %custom-call.7 = f32[1,128,128]{1,2,0:T(8,128)S(1)} custom-call(f32[1,128,128]{2,1,0:T(8,128)S(1)} %get-tuple-element.6), custom_call_target="InvertDiagBlocksLowerTriangular" | custom-call | tf_op jit(solution)/shard_map/jit(_solve_triangular)/triangular_solve | solution.py:50
  321.3 1.8 copy.193
  323.1 1.1 convolution_bitcast_fusion
  324.5 1.0 concatenate.48
  328.2 78.9 %all-gather.13.cloned.1.call-done = f32[4096,128]{0,1:T(8,128)} async-done(((f32[128,128]{0,1:T(8,128)}), f32[4096,128]{0,1:T(8,128)}) %all-gather.13.cloned.1.call-update) | async-done | bytes 2097168 | tf_op jit(solution)/shard_map/all_gather | solution.py:90
  407.2 2.1 copy.205
  409.6 1.8 fusion
  411.6 3.6 copy.198
  (171 shorter events, 23.0 us)
Async XLA Ops:
  6.5 119.4 %all-gather.7.cloned.1.call-start = ((), (), s32[]{:S(2)}) async-start(), calls=%async_computation | async-start | bytes 1114112 | tf_op jit(solution)/shard_map/all_gather | solution.py:77
  11.8 196.2 %all-gather.9.cloned.1.call-start = ((), (), s32[]{:S(2)}) async-start(), calls=%async_computation.1 | async-start | bytes 2162688 | tf_op jit(solution)/shard_map/all_gather | solution.py:90
  11.8 9.8 %collective-permute-start = (f32[4,8]{0,1:T(8,128)S(1)}, f32[4,8]{0,1:T(8,128)S(1)}, u32[]{:S(2)}, u32[]{:S(2)}) collective-permute-start(f32[4,8]{0,1:T(8,128)S(1)} %slice.64), channel_id=1, source_target_pairs={{0,1},{1,2},{2,3},{3,4},{4,5},{5,6},{6,7},{7,8},{8,9},{9,10},{10,1... | collective-permute-start | bytes 392 | tf_op jit(solution)/shard_map/ppermute | solution.py:19
  11.9 10.0 %collective-permute-start.1 = (f32[4,8]{0,1:T(8,128)S(1)}, f32[4,8]{0,1:T(8,128)S(1)}, u32[]{:S(2)}, u32[]{:S(2)}) collective-permute-start(f32[4,8]{0,1:T(8,128)S(1)} %slice.64), channel_id=1, source_target_pairs={{0,15},{1,0},{2,1},{3,2},{4,3},{5,4},{6,5},{7,6},{8,7},{9,8},{10,9... | collective-permute-start | bytes 392 | tf_op jit(solution)/shard_map/ppermute | solution.py:28
  21.9 4.3 %collective-permute-start.2 = (f32[4,8]{0,1:T(8,128)S(1)}, f32[4,8]{0,1:T(8,128)S(1)}, u32[]{:S(2)}, u32[]{:S(2)}) collective-permute-start(f32[4,8]{0,1:T(8,128)S(1)} %collective-permute-done), channel_id=1, source_target_pairs={{0,1},{1,2},{2,3},{3,4},{4,5},{5,6},{6,7},{7,8},{8,9},{9,10},{10,1... | collective-permute-start | bytes 392 | tf_op jit(solution)/shard_map/ppermute | solution.py:19
  22.2 4.2 %collective-permute-start.3 = (f32[4,8]{0,1:T(8,128)S(1)}, f32[4,8]{0,1:T(8,128)S(1)}, u32[]{:S(2)}, u32[]{:S(2)}) collective-permute-start(f32[4,8]{0,1:T(8,128)S(1)} %collective-permute-done.1), channel_id=1, source_target_pairs={{0,15},{1,0},{2,1},{3,2},{4,3},{5,4},{6,5},{7,6},{8,7},{9,8},{10,9... | collective-permute-start | bytes 392 | tf_op jit(solution)/shard_map/ppermute | solution.py:28
  26.4 4.3 %collective-permute-start.4 = (f32[4,8]{0,1:T(8,128)S(1)}, f32[4,8]{0,1:T(8,128)S(1)}, u32[]{:S(2)}, u32[]{:S(2)}) collective-permute-start(f32[4,8]{0,1:T(8,128)S(1)} %collective-permute-done.2), channel_id=1, source_target_pairs={{0,1},{1,2},{2,3},{3,4},{4,5},{5,6},{6,7},{7,8},{8,9},{9,10},{10,1... | collective-permute-start | bytes 392 | tf_op jit(solution)/shard_map/ppermute | solution.py:19
  26.7 4.3 %collective-permute-start.5 = (f32[4,8]{0,1:T(8,128)S(1)}, f32[4,8]{0,1:T(8,128)S(1)}, u32[]{:S(2)}, u32[]{:S(2)}) collective-permute-start(f32[4,8]{0,1:T(8,128)S(1)} %collective-permute-done.3), channel_id=1, source_target_pairs={{0,15},{1,0},{2,1},{3,2},{4,3},{5,4},{6,5},{7,6},{8,7},{9,8},{10,9... | collective-permute-start | bytes 392 | tf_op jit(solution)/shard_map/ppermute | solution.py:28
  30.9 4.3 %collective-permute-start.6 = (f32[4,8]{0,1:T(8,128)S(1)}, f32[4,8]{0,1:T(8,128)S(1)}, u32[]{:S(2)}, u32[]{:S(2)}) collective-permute-start(f32[4,8]{0,1:T(8,128)S(1)} %collective-permute-done.4), channel_id=1, source_target_pairs={{0,1},{1,2},{2,3},{3,4},{4,5},{5,6},{6,7},{7,8},{8,9},{9,10},{10,1... | collective-permute-start | bytes 392 | tf_op jit(solution)/shard_map/ppermute | solution.py:19
  31.2 4.2 %collective-permute-start.7 = (f32[4,8]{0,1:T(8,128)S(1)}, f32[4,8]{0,1:T(8,128)S(1)}, u32[]{:S(2)}, u32[]{:S(2)}) collective-permute-start(f32[4,8]{0,1:T(8,128)S(1)} %collective-permute-done.5), channel_id=1, source_target_pairs={{0,15},{1,0},{2,1},{3,2},{4,3},{5,4},{6,5},{7,6},{8,7},{9,8},{10,9... | collective-permute-start | bytes 392 | tf_op jit(solution)/shard_map/ppermute | solution.py:28
  35.5 4.2 %collective-permute-start.8 = (f32[4,8]{0,1:T(8,128)S(1)}, f32[4,8]{0,1:T(8,128)S(1)}, u32[]{:S(2)}, u32[]{:S(2)}) collective-permute-start(f32[4,8]{0,1:T(8,128)S(1)} %collective-permute-done.6), channel_id=1, source_target_pairs={{0,1},{1,2},{2,3},{3,4},{4,5},{5,6},{6,7},{7,8},{8,9},{9,10},{10,1... | collective-permute-start | bytes 392 | tf_op jit(solution)/shard_map/ppermute | solution.py:19
  35.8 4.2 %collective-permute-start.9 = (f32[4,8]{0,1:T(8,128)S(1)}, f32[4,8]{0,1:T(8,128)S(1)}, u32[]{:S(2)}, u32[]{:S(2)}) collective-permute-start(f32[4,8]{0,1:T(8,128)S(1)} %collective-permute-done.7), channel_id=1, source_target_pairs={{0,15},{1,0},{2,1},{3,2},{4,3},{5,4},{6,5},{7,6},{8,7},{9,8},{10,9... | collective-permute-start | bytes 392 | tf_op jit(solution)/shard_map/ppermute | solution.py:28
  40.0 4.2 %collective-permute-start.10 = (f32[4,8]{0,1:T(8,128)S(1)}, f32[4,8]{0,1:T(8,128)S(1)}, u32[]{:S(2)}, u32[]{:S(2)}) collective-permute-start(f32[4,8]{0,1:T(8,128)S(1)} %collective-permute-done.8), channel_id=1, source_target_pairs={{0,1},{1,2},{2,3},{3,4},{4,5},{5,6},{6,7},{7,8},{8,9},{9,10},{10,1... | collective-permute-start | bytes 392 | tf_op jit(solution)/shard_map/ppermute | solution.py:19
  40.3 4.3 %collective-permute-start.11 = (f32[4,8]{0,1:T(8,128)S(1)}, f32[4,8]{0,1:T(8,128)S(1)}, u32[]{:S(2)}, u32[]{:S(2)}) collective-permute-start(f32[4,8]{0,1:T(8,128)S(1)} %collective-permute-done.9), channel_id=1, source_target_pairs={{0,15},{1,0},{2,1},{3,2},{4,3},{5,4},{6,5},{7,6},{8,7},{9,8},{10,9... | collective-permute-start | bytes 392 | tf_op jit(solution)/shard_map/ppermute | solution.py:28
  44.5 4.3 %collective-permute-start.12 = (f32[4,8]{0,1:T(8,128)S(1)}, f32[4,8]{0,1:T(8,128)S(1)}, u32[]{:S(2)}, u32[]{:S(2)}) collective-permute-start(f32[4,8]{0,1:T(8,128)S(1)} %collective-permute-done.10), channel_id=1, source_target_pairs={{0,1},{1,2},{2,3},{3,4},{4,5},{5,6},{6,7},{7,8},{8,9},{9,10},{10,1... | collective-permute-start | bytes 392 | tf_op jit(solution)/shard_map/ppermute | solution.py:19
  44.8 4.6 %collective-permute-start.13 = (f32[4,8]{0,1:T(8,128)S(1)}, f32[4,8]{0,1:T(8,128)S(1)}, u32[]{:S(2)}, u32[]{:S(2)}) collective-permute-start(f32[4,8]{0,1:T(8,128)S(1)} %collective-permute-done.11), channel_id=1, source_target_pairs={{0,15},{1,0},{2,1},{3,2},{4,3},{5,4},{6,5},{7,6},{8,7},{9,8},{10,9... | collective-permute-start | bytes 392 | tf_op jit(solution)/shard_map/ppermute | solution.py:28
  49.0 4.2 %collective-permute-start.14 = (f32[4,8]{0,1:T(8,128)S(1)}, f32[4,8]{0,1:T(8,128)S(1)}, u32[]{:S(2)}, u32[]{:S(2)}) collective-permute-start(f32[4,8]{0,1:T(8,128)S(1)} %collective-permute-done.12), channel_id=1, source_target_pairs={{0,1},{1,2},{2,3},{3,4},{4,5},{5,6},{6,7},{7,8},{8,9},{9,10},{10,1... | collective-permute-start | bytes 392 | tf_op jit(solution)/shard_map/ppermute | solution.py:19
  129.9 191.4 %all-gather.11.cloned.1.call-start = ((), (), s32[]{:S(2)}) async-start(), calls=%async_computation.2 | async-start | bytes 1114112 | tf_op jit(solution)/shard_map/all_gather | solution.py:77
  212.1 1.3 copy-start
  214.1 193.1 %all-gather.13.cloned.1.call-start = ((), (), s32[]{:S(2)}) async-start(), calls=%async_computation.3 | async-start | bytes 2162688 | tf_op jit(solution)/shard_map/all_gather | solution.py:90
  215.2 4.2 %collective-permute-start.15 = (f32[4,8]{0,1:T(8,128)S(1)}, f32[4,8]{0,1:T(8,128)S(1)}, u32[]{:S(2)}, u32[]{:S(2)}) collective-permute-start(f32[4,8]{0,1:T(8,128)S(1)} %slice.69), channel_id=1, source_target_pairs={{0,1},{1,2},{2,3},{3,4},{4,5},{5,6},{6,7},{7,8},{8,9},{9,10},{10,1... | collective-permute-start | bytes 392 | tf_op jit(solution)/shard_map/ppermute | solution.py:19
  215.3 4.4 %collective-permute-start.16 = (f32[4,8]{0,1:T(8,128)S(1)}, f32[4,8]{0,1:T(8,128)S(1)}, u32[]{:S(2)}, u32[]{:S(2)}) collective-permute-start(f32[4,8]{0,1:T(8,128)S(1)} %slice.69), channel_id=1, source_target_pairs={{0,15},{1,0},{2,1},{3,2},{4,3},{5,4},{6,5},{7,6},{8,7},{9,8},{10,9... | collective-permute-start | bytes 392 | tf_op jit(solution)/shard_map/ppermute | solution.py:28
  219.8 4.3 %collective-permute-start.17 = (f32[4,8]{0,1:T(8,128)S(1)}, f32[4,8]{0,1:T(8,128)S(1)}, u32[]{:S(2)}, u32[]{:S(2)}) collective-permute-start(f32[4,8]{0,1:T(8,128)S(1)} %collective-permute-done.15), channel_id=1, source_target_pairs={{0,1},{1,2},{2,3},{3,4},{4,5},{5,6},{6,7},{7,8},{8,9},{9,10},{10,1... | collective-permute-start | bytes 392 | tf_op jit(solution)/shard_map/ppermute | solution.py:19
  220.0 4.2 %collective-permute-start.18 = (f32[4,8]{0,1:T(8,128)S(1)}, f32[4,8]{0,1:T(8,128)S(1)}, u32[]{:S(2)}, u32[]{:S(2)}) collective-permute-start(f32[4,8]{0,1:T(8,128)S(1)} %collective-permute-done.16), channel_id=1, source_target_pairs={{0,15},{1,0},{2,1},{3,2},{4,3},{5,4},{6,5},{7,6},{8,7},{9,8},{10,9... | collective-permute-start | bytes 392 | tf_op jit(solution)/shard_map/ppermute | solution.py:28
  224.3 4.3 %collective-permute-start.19 = (f32[4,8]{0,1:T(8,128)S(1)}, f32[4,8]{0,1:T(8,128)S(1)}, u32[]{:S(2)}, u32[]{:S(2)}) collective-permute-start(f32[4,8]{0,1:T(8,128)S(1)} %collective-permute-done.17), channel_id=1, source_target_pairs={{0,1},{1,2},{2,3},{3,4},{4,5},{5,6},{6,7},{7,8},{8,9},{9,10},{10,1... | collective-permute-start | bytes 392 | tf_op jit(solution)/shard_map/ppermute | solution.py:19
  224.6 4.3 %collective-permute-start.20 = (f32[4,8]{0,1:T(8,128)S(1)}, f32[4,8]{0,1:T(8,128)S(1)}, u32[]{:S(2)}, u32[]{:S(2)}) collective-permute-start(f32[4,8]{0,1:T(8,128)S(1)} %collective-permute-done.18), channel_id=1, source_target_pairs={{0,15},{1,0},{2,1},{3,2},{4,3},{5,4},{6,5},{7,6},{8,7},{9,8},{10,9... | collective-permute-start | bytes 392 | tf_op jit(solution)/shard_map/ppermute | solution.py:28
  228.8 4.2 %collective-permute-start.21 = (f32[4,8]{0,1:T(8,128)S(1)}, f32[4,8]{0,1:T(8,128)S(1)}, u32[]{:S(2)}, u32[]{:S(2)}) collective-permute-start(f32[4,8]{0,1:T(8,128)S(1)} %collective-permute-done.19), channel_id=1, source_target_pairs={{0,1},{1,2},{2,3},{3,4},{4,5},{5,6},{6,7},{7,8},{8,9},{9,10},{10,1... | collective-permute-start | bytes 392 | tf_op jit(solution)/shard_map/ppermute | solution.py:19
  229.1 4.2 %collective-permute-start.22 = (f32[4,8]{0,1:T(8,128)S(1)}, f32[4,8]{0,1:T(8,128)S(1)}, u32[]{:S(2)}, u32[]{:S(2)}) collective-permute-start(f32[4,8]{0,1:T(8,128)S(1)} %collective-permute-done.20), channel_id=1, source_target_pairs={{0,15},{1,0},{2,1},{3,2},{4,3},{5,4},{6,5},{7,6},{8,7},{9,8},{10,9... | collective-permute-start | bytes 392 | tf_op jit(solution)/shard_map/ppermute | solution.py:28
  233.3 4.2 %collective-permute-start.23 = (f32[4,8]{0,1:T(8,128)S(1)}, f32[4,8]{0,1:T(8,128)S(1)}, u32[]{:S(2)}, u32[]{:S(2)}) collective-permute-start(f32[4,8]{0,1:T(8,128)S(1)} %collective-permute-done.21), channel_id=1, source_target_pairs={{0,1},{1,2},{2,3},{3,4},{4,5},{5,6},{6,7},{7,8},{8,9},{9,10},{10,1... | collective-permute-start | bytes 392 | tf_op jit(solution)/shard_map/ppermute | solution.py:19
  233.6 4.2 %collective-permute-start.24 = (f32[4,8]{0,1:T(8,128)S(1)}, f32[4,8]{0,1:T(8,128)S(1)}, u32[]{:S(2)}, u32[]{:S(2)}) collective-permute-start(f32[4,8]{0,1:T(8,128)S(1)} %collective-permute-done.22), channel_id=1, source_target_pairs={{0,15},{1,0},{2,1},{3,2},{4,3},{5,4},{6,5},{7,6},{8,7},{9,8},{10,9... | collective-permute-start | bytes 392 | tf_op jit(solution)/shard_map/ppermute | solution.py:28
  237.8 4.3 %collective-permute-start.25 = (f32[4,8]{0,1:T(8,128)S(1)}, f32[4,8]{0,1:T(8,128)S(1)}, u32[]{:S(2)}, u32[]{:S(2)}) collective-permute-start(f32[4,8]{0,1:T(8,128)S(1)} %collective-permute-done.23), channel_id=1, source_target_pairs={{0,1},{1,2},{2,3},{3,4},{4,5},{5,6},{6,7},{7,8},{8,9},{9,10},{10,1... | collective-permute-start | bytes 392 | tf_op jit(solution)/shard_map/ppermute | solution.py:19
  238.2 4.3 %collective-permute-start.26 = (f32[4,8]{0,1:T(8,128)S(1)}, f32[4,8]{0,1:T(8,128)S(1)}, u32[]{:S(2)}, u32[]{:S(2)}) collective-permute-start(f32[4,8]{0,1:T(8,128)S(1)} %collective-permute-done.24), channel_id=1, source_target_pairs={{0,15},{1,0},{2,1},{3,2},{4,3},{5,4},{6,5},{7,6},{8,7},{9,8},{10,9... | collective-permute-start | bytes 392 | tf_op jit(solution)/shard_map/ppermute | solution.py:28
  242.4 4.2 %collective-permute-start.27 = (f32[4,8]{0,1:T(8,128)S(1)}, f32[4,8]{0,1:T(8,128)S(1)}, u32[]{:S(2)}, u32[]{:S(2)}) collective-permute-start(f32[4,8]{0,1:T(8,128)S(1)} %collective-permute-done.25), channel_id=1, source_target_pairs={{0,1},{1,2},{2,3},{3,4},{4,5},{5,6},{6,7},{7,8},{8,9},{9,10},{10,1... | collective-permute-start | bytes 392 | tf_op jit(solution)/shard_map/ppermute | solution.py:19
  242.7 4.3 %collective-permute-start.28 = (f32[4,8]{0,1:T(8,128)S(1)}, f32[4,8]{0,1:T(8,128)S(1)}, u32[]{:S(2)}, u32[]{:S(2)}) collective-permute-start(f32[4,8]{0,1:T(8,128)S(1)} %collective-permute-done.26), channel_id=1, source_target_pairs={{0,15},{1,0},{2,1},{3,2},{4,3},{5,4},{6,5},{7,6},{8,7},{9,8},{10,9... | collective-permute-start | bytes 392 | tf_op jit(solution)/shard_map/ppermute | solution.py:28
  246.9 4.2 %collective-permute-start.29 = (f32[4,8]{0,1:T(8,128)S(1)}, f32[4,8]{0,1:T(8,128)S(1)}, u32[]{:S(2)}, u32[]{:S(2)}) collective-permute-start(f32[4,8]{0,1:T(8,128)S(1)} %collective-permute-done.27), channel_id=1, source_target_pairs={{0,1},{1,2},{2,3},{3,4},{4,5},{5,6},{6,7},{7,8},{8,9},{9,10},{10,1... | collective-permute-start | bytes 392 | tf_op jit(solution)/shard_map/ppermute | solution.py:19
  325.5 2.7 copy-start.2
  407.2 2.4 copy-start.1
  407.2 2.5 copy-start.3
Sparse Core Ops, SparseCore 0:
  11.9 46.5 all-gather.6
  130.0 77.8 all-gather.8
  214.2 41.1 all-gather.10
  326.4 80.7 all-gather.12
